TPU v7x, 32 devices: a whole 2x2x4 slice. The times are simulated.
32 devices in a mesh: clips: 2 (over y), seq: 4 (over z), tp: 2 (over x), dp: 2 (over core).
Axes of the slice: x: 2, y: 2, z: 4, core: 2. Of those that a mesh axis runs over, the one named last changes fastest.
Arguments:
- video_query: bfloat16 [4, 512, 4096], P(('clips', 'dp'), 'seq', 'tp'), parts along dimension 0, may hold values from -384 to 384
- video_key: bfloat16 [4, 512, 4096], P(('clips', 'dp'), 'seq', 'tp'), parts along dimension 0, may hold values from -384 to 384
- video_value: bfloat16 [4, 512, 4096], P(('clips', 'dp'), 'seq', 'tp'), parts along dimension 0, may hold values from -6 to 6
- cross_query: bfloat16 [4, 512, 2048], P(('clips', 'dp'), 'seq', 'tp'), parts along dimension 0, may hold values from -384 to 384
- audio_key: bfloat16 [4, 32, 2048], P(('clips', 'dp'), 'seq', 'tp'), parts along dimension 0, may hold values from -384 to 384
- audio_value: bfloat16 [4, 32, 2048], P(('clips', 'dp'), 'seq', 'tp'), parts along dimension 0, may hold values from -6 to 6
- audio_query: bfloat16 [4, 32, 2048], P(('clips', 'dp'), 'seq', 'tp'), parts along dimension 0, may hold values from -384 to 384
- cross_key: bfloat16 [4, 512, 2048], P(('clips', 'dp'), 'seq', 'tp'), parts along dimension 0, may hold values from -384 to 384
- cross_value: bfloat16 [4, 512, 2048], P(('clips', 'dp'), 'seq', 'tp'), parts along dimension 0, may hold values from -6 to 6
- audio_input: bfloat16 [4, 32, 2048], P(('clips', 'dp'), 'seq'), parts along dimension 0, may hold values from -0.29882812 to 0.29882812
- norm_gain: float32 [2048], replicated, may hold values from 0.1 to 1.9
- up_weight: bfloat16 [2048, 8192], P('tp', 'seq'), may hold values from -0.125 to 0.125
- down_weight: bfloat16 [8192, 2048], P('seq', 'tp'), may hold values from -0.0625 to 0.0625
Outputs:
- video_mixed: bfloat16 [4, 512, 4096], P(('clips', 'dp'), 'seq', 'tp'), parts along dimension 0
- video_heard: bfloat16 [4, 512, 2048], P(('clips', 'dp'), 'seq', 'tp'), parts along dimension 0
- audio_seen: bfloat16 [4, 32, 2048], P(('clips', 'dp'), 'seq', 'tp'), parts along dimension 0
- audio_mlp: bfloat16 [4, 32, 2048], P(('clips', 'dp'), 'seq', 'tp'), parts along dimension 0
There are 2 independent parts, one for each index of `clips`. A program takes and returns all parts, laid end to end along the dimension named above; an argument that names none is the same for every part. Nothing has to cross between parts.
All inputs are finite; a program needn't handle non-finite values.
Results may differ from a plain program's by a relative error of at most 0.013.
Values may be sent and summed in bfloat16 or wider, within the bound.
A program may use at most 64 MiB of HBM per device.

v0:
```python
import math
import jax
import jax.numpy as jnp
from jax import lax
from jax.sharding import PartitionSpec as P

VHEAD = 128
CHEAD = 64


def attend_rows(queries, keys_in, values_in, head_count):
    head_size = queries.shape[1] // head_count
    query_heads = queries.reshape(queries.shape[0], head_count, head_size)
    key_heads = keys_in.reshape(keys_in.shape[0], head_count, head_size)
    value_heads = values_in.reshape(values_in.shape[0], head_count, head_size)
    scores = jnp.einsum(
        "qhd,khd->qhk", query_heads, key_heads, preferred_element_type=jnp.float32
    ) / math.sqrt(head_size)
    peak_value = jnp.max(scores, axis=2, keepdims=True)
    weights = jnp.exp(scores - peak_value)
    totals = jnp.sum(weights, axis=2)
    weighted = jnp.einsum(
        "qhk,khd->qhd",
        weights.astype(jnp.bfloat16),
        value_heads,
        preferred_element_type=jnp.float32,
    )
    result = weighted / totals[:, :, None]
    return result.reshape(queries.shape[0], head_count * head_size).astype(jnp.bfloat16)


def attend(queries, keys_in, values_in, head_count):
    row_total = queries.shape[0]
    block_rows = 512 if row_total % 512 == 0 else row_total
    pieces = queries.reshape(row_total // block_rows, block_rows, queries.shape[1])
    result = lax.map(
        lambda row_piece: attend_rows(row_piece, keys_in, values_in, head_count), pieces
    )
    return result.reshape(row_total, queries.shape[1])


def video_self(queries, keys_in, values_in):
    seq_count = lax.axis_size("seq")
    local_heads = queries.shape[1] // VHEAD
    dest_heads = max(local_heads // seq_count, 1)
    blocks = seq_count * dest_heads // local_heads
    groups = local_heads // dest_heads
    group_width = dest_heads * VHEAD
    token_count = queries.shape[0]
    block_tokens = token_count // blocks

    def spread(tensor):
        shaped = tensor.reshape(token_count, groups, group_width).transpose(1, 0, 2)
        shaped = jnp.broadcast_to(shaped[:, None], (groups, blocks, token_count, group_width))
        return shaped.reshape(seq_count, token_count, group_width)

    shaped = queries.reshape(blocks, block_tokens, groups, group_width).transpose(2, 0, 1, 3)
    own_queries = lax.all_to_all(
        shaped.reshape(seq_count, block_tokens, group_width),
        "seq",
        split_axis=0,
        concat_axis=0,
        tiled=True,
    )
    keys_all = lax.all_to_all(spread(keys_in), "seq", split_axis=0, concat_axis=0, tiled=True)
    values_all = lax.all_to_all(spread(values_in), "seq", split_axis=0, concat_axis=0, tiled=True)
    keys_all = keys_all.reshape(-1, group_width)
    values_all = values_all.reshape(-1, group_width)
    own_queries = own_queries.reshape(-1, group_width)
    attended = attend(own_queries, keys_all, values_all, dest_heads)
    returned = lax.all_to_all(
        attended.reshape(seq_count, block_tokens, group_width),
        "seq",
        split_axis=0,
        concat_axis=0,
        tiled=True,
    )
    returned = returned.reshape(groups, blocks, block_tokens, group_width).transpose(1, 2, 0, 3)
    return returned.reshape(token_count, groups * group_width)


def audio_listen(queries, keys_in, values_in, head_count):
    head_size = queries.shape[1] // head_count
    query_heads = queries.reshape(queries.shape[0], head_count, head_size)
    key_heads = keys_in.reshape(keys_in.shape[0], head_count, head_size)
    value_heads = values_in.reshape(values_in.shape[0], head_count, head_size)
    scores = jnp.einsum(
        "qhd,khd->qhk", query_heads, key_heads, preferred_element_type=jnp.float32
    ) / math.sqrt(head_size)
    local_peak = jnp.max(scores, axis=2)
    peak_value = lax.pmax(local_peak, "seq")
    weights = jnp.exp(scores - peak_value[:, :, None])
    totals = jnp.sum(weights, axis=2)
    weighted = jnp.einsum(
        "qhk,khd->qhd",
        weights.astype(jnp.bfloat16),
        value_heads,
        preferred_element_type=jnp.float32,
    )
    totals, weighted = (totals, weighted.reshape(queries.shape[0], head_count * head_size))
    totals, weighted = (
        lax.psum_scatter(totals, "seq", scatter_dimension=0, tiled=True),
        lax.psum_scatter(weighted, "seq", scatter_dimension=0, tiled=True),
    )
    return (weighted / jnp.repeat(totals, head_size, axis=1)).astype(jnp.bfloat16)


def audio_block(audio_rows, audio_seen, norm_gain, up_weight, down_weight):
    features = lax.all_gather(audio_seen, "tp", axis=1, tiled=True)
    residual = audio_rows.astype(jnp.float32) + features.astype(jnp.float32)
    scale_factor = lax.rsqrt(jnp.mean(residual * residual, axis=1, keepdims=True) + 1e-06)
    normed = (residual * scale_factor * norm_gain).astype(jnp.bfloat16)
    slice_width = up_weight.shape[0]
    own_features = lax.dynamic_slice_in_dim(
        normed, lax.axis_index("tp") * slice_width, slice_width, 1
    )
    partial_sum = jnp.dot(
        lax.all_gather(own_features, "seq", axis=0, tiled=True),
        up_weight,
        preferred_element_type=jnp.float32,
    )
    hidden = jax.nn.gelu(lax.psum(partial_sum, "tp")).astype(jnp.bfloat16)
    return lax.psum_scatter(
        jnp.dot(hidden, down_weight, preferred_element_type=jnp.float32),
        "seq",
        scatter_dimension=0,
        tiled=True,
    ).astype(jnp.bfloat16)


def body(
    video_query,
    video_key,
    video_value,
    cross_query,
    audio_key,
    audio_value,
    audio_query,
    cross_key,
    cross_value,
    audio_input,
    norm_gain,
    up_weight,
    down_weight,
):
    mixed_list, heard_list, seen_list, output_list = ([], [], [], [])
    cross_heads = cross_query.shape[2] // CHEAD
    mixed_list.append(video_self(video_query[0], video_key[0], video_value[0]))
    gathered_query = lax.all_gather(audio_query[0], "seq", axis=0, tiled=True)
    gathered_key = lax.all_gather(audio_key[0], "seq", axis=0, tiled=True)
    gathered_value = lax.all_gather(audio_value[0], "seq", axis=0, tiled=True)
    heard_list.append(attend(cross_query[0], gathered_key, gathered_value, cross_heads))
    audio_seen = audio_listen(gathered_query, cross_key[0], cross_value[0], cross_heads)
    seen_list.append(audio_seen)
    output_list.append(audio_block(audio_input[0], audio_seen, norm_gain, up_weight, down_weight))
    return (
        jnp.stack(mixed_list),
        jnp.stack(heard_list),
        jnp.stack(seen_list),
        jnp.stack(output_list),
    )


def solution(mesh):
    placed = (
        P(("clips", "dp"), "seq", "tp"),
        P(("clips", "dp"), "seq", "tp"),
        P(("clips", "dp"), "seq", "tp"),
        P(("clips", "dp"), "seq", "tp"),
        P(("clips", "dp"), "seq", "tp"),
        P(("clips", "dp"), "seq", "tp"),
        P(("clips", "dp"), "seq", "tp"),
        P(("clips", "dp"), "seq", "tp"),
        P(("clips", "dp"), "seq", "tp"),
        P(("clips", "dp"), "seq", None),
        P(),
        P("tp", "seq"),
        P("seq", "tp"),
    )
    return jax.shard_map(
        body,
        mesh=mesh,
        in_specs=placed,
        out_specs=(
            P(("clips", "dp"), "seq", "tp"),
            P(("clips", "dp"), "seq", "tp"),
            P(("clips", "dp"), "seq", "tp"),
            P(("clips", "dp"), "seq", "tp"),
        ),
        check_vma=False,
    )
```

profile of v0, /device:TPU:0, one launch (start us, length us, event | category | flops | bytes accessed | tf_op | source)
XLA Modules:
  0.0 171.0 jit_solution(16451558797304456168)
XLA Ops:
  7.2 2.0 %copy.100 = bf16[1,16,4,8,512]{4,3,1,2,0:T(8,128)(2,1)} copy(bf16[1,16,4,8,512]{4,3,2,1,0:T(8,128)(2,1)} %bitcast.77) | data formatting | bytes 1048576 | tf_op jit(solution)/shard_map/reshape;squeeze | solution.py:57
  9.2 6.3 %all-to-all-start.1 = ((bf16[4,128,512]{2,1,0:T(8,128)(2,1)}), bf16[4,128,512]{2,1,0:T(8,128)(2,1)S(1)}, u32[]{:S(2)}, u32[]{:S(2)}) async-start(bf16[4,128,512]{2,1,0:T(8,128)(2,1)} %bitcast.69), calls=%async_computation.1 | async-start | bytes 1048576 | tf_op jit(solution)/shard_map/all_to_all | solution.py:58
  15.5 0.0 reduce-scatter.3.cloned.1.call-start
  15.5 1.2 copy.70
  16.7 1.1 copy.68
  17.8 0.0 copy-start.9
  17.8 0.0 copy-start.8
  17.9 17.8 %all-gather.2 = bf16[1,32,1024]{2,1,0:T(8,128)(2,1)S(1)} all-gather(bf16[1,8,1024]{2,1,0:T(8,128)(2,1)} %param.19), channel_id=4, replica_groups=mesh['clips'=2,'seq'=4,'tp'=2,'dp'=2] {'seq'}, dimensions={1}, use_global_device_ids=true | all-gather | bytes 81920 | tf_op jit(solution)/shard_map/all_gather | solution.py:149
  35.7 0.1 reshape.82
  35.8 0.3 fusion.57
  36.1 11.0 %pmax.7 = f32[32,16]{0,1:T(8,128)S(1)} all-reduce(f32[32,16]{0,1:T(8,128)S(1)} %get-tuple-element.56), channel_id=1, replica_groups=mesh['clips'=2,'seq'=4,'tp'=2,'dp'=2] {'seq'}, use_global_device_ids=true, to_apply=%region_5.6 | all-reduce | flops 512 | bytes 4096 | tf_op jit(solution)/shard_map/pmax | solution.py:91
  47.2 0.3 convolution_bitcast_fusion.1
  47.5 0.2 copy.71
  47.6 0.8 reshape.83
  48.4 0.0 reduce-scatter.3.cloned.1.call-update
  48.5 0.4 reshape_squeeze.15
  48.9 0.9 copy.102
  49.7 0.4 reshape_squeeze.17
  50.1 0.9 copy.101
  51.0 0.2 copy.65
  51.2 13.2 %all-gather = bf16[1,32,1024]{2,1,0:T(8,128)(2,1)S(1)} all-gather(bf16[1,8,1024]{2,1,0:T(8,128)(2,1)S(1)} %copy-done.6), channel_id=2, replica_groups=mesh['clips'=2,'seq'=4,'tp'=2,'dp'=2] {'seq'}, dimensions={1}, use_global_device_ids=true | all-gather | bytes 81920 | tf_op jit(solution)/shard_map/all_gather | solution.py:150
  64.4 0.1 reshape.79
  64.5 0.3 fusion.34
  64.8 0.1 copy.72
  64.9 0.6 dynamic-slice
  66.1 15.7 %all-reduce = f32[32,16]{1,0:T(8,128)S(1)} all-reduce(f32[32,16]{1,0:T(8,128)S(1)} %copy.72), channel_id=6, replica_groups=mesh['clips'=2,'seq'=4,'tp'=2,'dp'=2] {'seq'}, use_global_device_ids=true, to_apply=%region_8.9.clone | all-reduce | flops 512 | bytes 4096
  81.8 0.1 broadcast_in_dim.16
  81.9 0.1 reshape.84
  82.0 0.2 fusion.56
  82.2 0.1 fusion.32
  82.3 3.5 %all-to-all-start = ((bf16[4,128,512]{2,1,0:T(8,128)(2,1)}), bf16[4,128,512]{2,1,0:T(8,128)(2,1)S(1)}, u32[]{:S(2)}, u32[]{:S(2)}) async-start(bf16[4,128,512]{2,1,0:T(8,128)(2,1)} %bitcast.71), calls=%async_computation | async-start | bytes 1048576 | tf_op jit(solution)/shard_map/all_to_all | solution.py:65
  85.8 0.0 reduce-scatter.3.cloned.1.call-done
  85.8 0.8 divide_convert_fusion
  86.6 0.0 copy-start.4
  86.6 4.4 %all_gather.18 = bf16[8,2048]{1,0:T(8,128)(2,1)S(1)} all-gather(bf16[8,1024]{1,0:T(8,128)(2,1)S(1)} %divide_convert_fusion), channel_id=1, replica_groups=mesh['clips'=2,'seq'=4,'tp'=2,'dp'=2] {'tp'}, dimensions={1}, use_global_device_ids=true | all-gather | bytes 49152 | tf_op jit(solution)/shard_map/all_gather | solution.py:109
  91.0 0.1 multiply_reduce_fusion
  91.2 0.1 fusion.50
  91.2 13.9 %all_gather.19 = bf16[32,1024]{1,0:T(8,128)(2,1)S(1)} all-gather(bf16[8,1024]{1,0:T(8,128)(2,1)S(1)} %fusion.50), channel_id=1, replica_groups=mesh['clips'=2,'seq'=4,'tp'=2,'dp'=2] {'seq'}, dimensions={0}, use_global_device_ids=true | all-gather | bytes 81920 | tf_op jit(solution)/shard_map/all_gather | solution.py:118
  105.1 4.6 %all-to-all-start.2 = ((bf16[4,128,512]{2,1,0:T(8,128)(2,1)}), bf16[4,128,512]{2,1,0:T(8,128)(2,1)S(1)}, u32[]{:S(2)}, u32[]{:S(2)}) async-start(bf16[4,128,512]{2,1,0:T(8,128)(2,1)} %bitcast.70), calls=%async_computation.2 | async-start | bytes 1048576 | tf_op jit(solution)/shard_map/all_to_all | solution.py:66
  109.7 3.7 %fusion.58 = f32[32,2048]{1,0:T(8,128)} fusion(bf16[32,1024]{1,0:T(8,128)(2,1)S(1)} %all_gather.19, bf16[1024,2048]{1,0:T(8,128)(2,1)} %param.24), kind=kOutput, calls=%fused_computation.67 | convolution fusion | flops 134217728 | bytes 4521984 | tf_op jit(solution)/shard_map/dot_general | solution.py:117
  113.4 0.0 all-reduce.3.cloned.1.call-update
  113.5 0.1 reshape.77
  113.6 0.1 reshape_reshape.10
  113.7 0.7 bitcast_reduce_fusion
  114.5 1.9 %copy-done = f32[4,512,512]{2,1,0:T(8,128)} copy-done((f32[4,512,512]{2,1,0:T(8,128)}, f32[4,512,512]{2,1,0:T(8,128)S(1)}, u32[]{:S(2)}) %copy-start) | copy-done | bytes 4194328
  116.4 0.7 fusion.1
  117.1 7.5 %all-to-all-done.2 = bf16[4,128,512]{2,1,0:T(8,128)(2,1)S(1)} async-done(((bf16[4,128,512]{2,1,0:T(8,128)(2,1)}), bf16[4,128,512]{2,1,0:T(8,128)(2,1)S(1)}, u32[]{:S(2)}, u32[]{:S(2)}) %all-to-all-start.2) | async-done | bytes 524320 | tf_op jit(solution)/shard_map/all_to_all | solution.py:66
  124.6 0.1 reshape_reshape.11
  124.8 3.4 %fusion.17 = bf16[512,4,128]{2,0,1:T(8,128)(2,1)S(1)} fusion(f32[4,512,512]{2,1,0:T(8,128)} %copy-done, f32[512,4]{0,1:T(4,128)S(1)} %get-tuple-element.52, bf16[512,4,128]{2,1,0:T(4,128)(2,1)S(1)} %reshape_reshape.11, f32[512,4]{0,1:T(4,128)S(1)} %fusion.1), kind=kOutput, calls=%fused_computation.18 | convolution fusion | flops 272105472 | bytes 5259264 | tf_op jit(solution)/shard_map/while/body/eval_jaxpr/qhk,khd->qhd/dot_general | solution.py:22
  128.2 0.4 copy.63
  128.6 1.0 convert_element_type.56
  129.6 3.5 %all-to-all-start.3 = ((bf16[4,128,512]{2,1,0:T(8,128)(2,1)}), bf16[4,128,512]{2,1,0:T(8,128)(2,1)S(1)}, u32[]{:S(2)}, u32[]{:S(2)}) async-start(bf16[4,128,512]{2,1,0:T(8,128)(2,1)} %convert_element_type.56), calls=%async_computation.3 | async-start | bytes 1048576 | tf_op jit(solution)/shard_map/all_to_all | solution.py:71
  133.0 0.0 reduce-scatter.5.cloned.1.call-start
  133.1 5.3 %all-reduce.3.cloned.1.call-done = f32[32,2048]{1,0:T(8,128)} async-done(((f32[32,2048]{1,0:T(8,128)}), f32[32,2048]{1,0:T(8,128)}) %all-reduce.3.cloned.1.call-update) | async-done | bytes 262160 | tf_op jit(solution)/shard_map/psum | solution.py:122
  138.4 3.7 %fusion.38 = f32[32,1024]{1,0:T(8,128)} fusion(bf16[2048,1024]{1,0:T(8,128)(2,1)} %param.25, f32[32,2048]{1,0:T(8,128)} %all-reduce.3.cloned.1.call-done), kind=kOutput, calls=%fused_computation.41 | convolution fusion | flops 134807552 | bytes 4587520 | tf_op jit(solution)/shard_map/dot_general | solution.py:124
  142.1 0.0 reduce-scatter.5.cloned.1.call-update
  142.1 13.3 %all-gather.1 = bf16[1,32,1024]{2,1,0:T(8,128)(2,1)S(1)} all-gather(bf16[1,8,1024]{2,1,0:T(8,128)(2,1)S(1)} %copy-done.7), channel_id=3, replica_groups=mesh['clips'=2,'seq'=4,'tp'=2,'dp'=2] {'seq'}, dimensions={1}, use_global_device_ids=true | all-gather | bytes 81920 | tf_op jit(solution)/shard_map/all_gather | solution.py:151
  155.4 0.1 reshape.81
  155.6 0.3 fusion.11
  155.8 0.9 copy.74
  156.7 5.1 %reduce-scatter.5.cloned.1.call-done = f32[8,1024]{1,0:T(8,128)} async-done(((f32[32,1024]{1,0:T(8,128)}), f32[8,1024]{1,0:T(8,128)}) %reduce-scatter.5.cloned.1.call-update) | async-done | bytes 32784 | tf_op jit(solution)/shard_map/reduce_scatter | solution.py:123
  161.8 1.4 convert_bitcast_fusion
  163.2 0.3 copy.64
  163.5 1.0 copy.73
  (23 shorter events, 0.1 us)
Async XLA Ops:
  7.2 41.3 %copy-start.1 = (bf16[1,128,2048]{2,1,0:T(8,128)(2,1)S(1)}, bf16[1,128,2048]{2,1,0:T(8,128)(2,1)}, u32[]{:S(2)}) copy-start(bf16[1,128,2048]{2,1,0:T(8,128)(2,1)} %param.14) | copy-start | bytes 1572868
  7.2 42.6 %copy-start.2 = (bf16[1,128,2048]{2,1,0:T(8,128)(2,1)S(1)}, bf16[1,128,2048]{2,1,0:T(8,128)(2,1)}, u32[]{:S(2)}) copy-start(bf16[1,128,2048]{2,1,0:T(8,128)(2,1)} %param.15) | copy-start | bytes 1572868
  9.2 73.1 %all-to-all-start.1 = ((bf16[4,128,512]{2,1,0:T(8,128)(2,1)}), bf16[4,128,512]{2,1,0:T(8,128)(2,1)S(1)}, u32[]{:S(2)}, u32[]{:S(2)}) async-start(bf16[4,128,512]{2,1,0:T(8,128)(2,1)} %bitcast.69), calls=%async_computation.1 | async-start | bytes 1048576 | tf_op jit(solution)/shard_map/all_to_all | solution.py:58
  15.5 35.5 %copy-start.3 = (bf16[1,128,1024]{2,1,0:T(8,128)(2,1)S(1)}, bf16[1,128,1024]{2,1,0:T(8,128)(2,1)}, u32[]{:S(2)}) copy-start(bf16[1,128,1024]{2,1,0:T(8,128)(2,1)} %param.16) | copy-start | bytes 786436
  15.5 35.7 %copy-start.6 = (bf16[1,8,1024]{2,1,0:T(8,128)(2,1)S(1)}, bf16[1,8,1024]{2,1,0:T(8,128)(2,1)}, u32[]{:S(2)}) copy-start(bf16[1,8,1024]{2,1,0:T(8,128)(2,1)} %param.17) | copy-start | bytes 49156
  15.5 70.3 %reduce-scatter.3.cloned.1.call-start = ((), (), s32[]{:S(2)}) async-start(), calls=%async_computation.6 | async-start | bytes 163840 | tf_op jit(solution)/shard_map/reduce_scatter | solution.py:103
  17.8 47.0 %copy-start.9 = (u32[32]{0:T(128)S(1)}, u32[32]{0:T(128)}, u32[]{:S(2)}) copy-start(u32[32]{0:T(128)} %constant.75) | copy-start | bytes 388
  17.8 64.2 %copy-start.8 = (f32[2048]{0:T(1024)S(1)}, f32[2048]{0:T(1024)}, u32[]{:S(2)}) copy-start(f32[2048]{0:T(1024)} %param.23) | copy-start | bytes 24580
  47.6 43.4 %copy-start.5 = (bf16[1,8,2048]{2,1,0:T(8,128)(2,1)S(1)}, bf16[1,8,2048]{2,1,0:T(8,128)(2,1)}, u32[]{:S(2)}) copy-start(bf16[1,8,2048]{2,1,0:T(8,128)(2,1)} %param.22) | copy-start | bytes 98308
  82.3 22.8 %all-to-all-start = ((bf16[4,128,512]{2,1,0:T(8,128)(2,1)}), bf16[4,128,512]{2,1,0:T(8,128)(2,1)S(1)}, u32[]{:S(2)}, u32[]{:S(2)}) async-start(bf16[4,128,512]{2,1,0:T(8,128)(2,1)} %bitcast.71), calls=%async_computation | async-start | bytes 1048576 | tf_op jit(solution)/shard_map/all_to_all | solution.py:65
  86.6 27.9 %copy-start.4 = (bf16[8,1024]{1,0:T(8,128)(2,1)}, bf16[8,1024]{1,0:T(8,128)(2,1)S(1)}, u32[]{:S(2)}) copy-start(bf16[8,1024]{1,0:T(8,128)(2,1)S(1)} %divide_convert_fusion) | copy-start | bytes 49156
  105.1 19.5 %all-to-all-start.2 = ((bf16[4,128,512]{2,1,0:T(8,128)(2,1)}), bf16[4,128,512]{2,1,0:T(8,128)(2,1)S(1)}, u32[]{:S(2)}, u32[]{:S(2)}) async-start(bf16[4,128,512]{2,1,0:T(8,128)(2,1)} %bitcast.70), calls=%async_computation.2 | async-start | bytes 1048576 | tf_op jit(solution)/shard_map/all_to_all | solution.py:66
  109.7 28.7 %all-reduce.3.cloned.1.call-start = ((), (), s32[]{:S(2)}) async-start(), calls=%async_computation.7 | async-start | bytes 524288 | tf_op jit(solution)/shard_map/psum | solution.py:122
  114.5 1.9 %copy-start = (f32[4,512,512]{2,1,0:T(8,128)}, f32[4,512,512]{2,1,0:T(8,128)S(1)}, u32[]{:S(2)}) copy-start(f32[4,512,512]{2,1,0:T(8,128)S(1)} %get-tuple-element.53) | copy-start | bytes 12582916
  128.1 14.0 %copy-start.7 = (bf16[1,8,1024]{2,1,0:T(8,128)(2,1)S(1)}, bf16[1,8,1024]{2,1,0:T(8,128)(2,1)}, u32[]{:S(2)}) copy-start(bf16[1,8,1024]{2,1,0:T(8,128)(2,1)} %param.18) | copy-start | bytes 49156
  129.6 33.6 %all-to-all-start.3 = ((bf16[4,128,512]{2,1,0:T(8,128)(2,1)}), bf16[4,128,512]{2,1,0:T(8,128)(2,1)S(1)}, u32[]{:S(2)}, u32[]{:S(2)}) async-start(bf16[4,128,512]{2,1,0:T(8,128)(2,1)} %convert_element_type.56), calls=%async_computation.3 | async-start | bytes 1048576 | tf_op jit(solution)/shard_map/all_to_all | solution.py:71
  133.0 28.8 %reduce-scatter.5.cloned.1.call-start = ((), (), s32[]{:S(2)}) async-start(), calls=%async_computation.8 | async-start | bytes 163840 | tf_op jit(solution)/shard_map/reduce_scatter | solution.py:123
Sparse Core Ops, SparseCore 0:
  48.6 17.6 reduce-scatter.2
  113.6 24.7 all-reduce.2
  142.2 19.5 reduce-scatter.4
where the time goes:
time: 172 us; the launch traced here: 171 us
  blocking collectives  89.4 us (52%)
  starting transfers between devices  18 us (10%)
  waiting for transfers between devices  18 us (10%)
  local copies, waits for them, and re-layouts  15 us (9%)
  between operations  14.7 us (9%)
  matrix products  12.6 us (7%)
  other arithmetic  3.38 us (2%)
    all_gather x1, blocking collectives, body(): gathered_query = lax.all_gather(audio_query[0], 'seq', axis=0, tiled=True)  17.8 us
    unnamed x1, blocking collectives  15.7 us
    all_gather x1, blocking collectives, audio_block(): lax.all_gather(own_features, 'seq', axis=0, tiled=True)  13.9 us
    all_gather x1, blocking collectives, body(): gathered_value = lax.all_gather(audio_value[0], 'seq', axis=0, tiled=True)  13.3 us
    all_gather x1, blocking collectives, body(): gathered_key = lax.all_gather(audio_key[0], 'seq', axis=0, tiled=True)  13.2 us
    pmax x1, blocking collectives, audio_listen(): peak_value = lax.pmax(local_peak, 'seq')  11 us
    all_to_all x1, waiting for transfers between devices, video_self(): lax.all_to_all(spread(values_in), 'seq', split_axis=0, concat_axis=0, til...  7.52 us
    unnamed x27, local copies, waits for them, and re-layouts  6.86 us
  transfers between devices with their start and end apart: 7, of which 3 were waited for; matrix products, arithmetic and copies ran while one was open for 15% of the time, Pallas kernels for 0%

commit v1 on v0

--- a/solution.py
+++ b/solution.py
@@ -6,6 +6,17 @@
 
 VHEAD = 128
 CHEAD = 64
+
+
+def turned_line(x, axis, along):
+    size = lax.axis_size(axis)
+    hops = [(i, (i + 1) % size) for i in range(size)]
+    shards = [x]
+    for stride in range(1, size):
+        shards = [lax.ppermute(shards[0], axis, hops), *shards]
+    full = jnp.concatenate(shards, axis=along)
+    turn = (lax.axis_index(axis) + 1) * shards[-1].shape[along]
+    return jnp.roll(full, turn, axis=along)
 
 
 def attend_rows(queries, keys_in, values_in, head_count):
@@ -146,7 +157,7 @@
     mixed_list, heard_list, seen_list, output_list = ([], [], [], [])
     cross_heads = cross_query.shape[2] // CHEAD
     mixed_list.append(video_self(video_query[0], video_key[0], video_value[0]))
-    gathered_query = lax.all_gather(audio_query[0], "seq", axis=0, tiled=True)
+    gathered_query = turned_line(audio_query[0], "seq", 0)
     gathered_key = lax.all_gather(audio_key[0], "seq", axis=0, tiled=True)
     gathered_value = lax.all_gather(audio_value[0], "seq", axis=0, tiled=True)
     heard_list.append(attend(cross_query[0], gathered_key, gathered_value, cross_heads))

time: 172 us -> 164 us (0.953)
  blocking collectives: 89.4 us -> 74.6 us
  starting transfers between devices: 18 us -> 21.5 us
  waiting for transfers between devices: 18 us -> 21.2 us
    all_gather x1 -> x0, blocking collectives: 17.8 us -> none  [body(): gathered_query = lax.all_gather(audio_query[0], 'seq', axis=0, tiled=True)]
    ppermute x0 -> x3, starting transfers between devices: none -> 6.05 us  [turned_line(): shards = [lax.ppermute(shards[0], axis, hops), *shards]]
    all_gather x1, blocking collectives: 13.2 us -> 17 us  [body(): gathered_key = lax.all_gather(audio_key[0], 'seq', axis=0, tiled=True)]
    ppermute x0 -> x3, waiting for transfers between devices: none -> 3.15 us  [turned_line(): shards = [lax.ppermute(shards[0], axis, hops), *shards]]
    all_to_all x1, starting transfers between devices: 6.35 us -> 3.86 us  [video_self(): lax.all_to_all(shaped.reshape(seq_count, block_tokens, group_width), 'seq...]
    unnamed x27 -> x34, local copies, waits for them, and re-layouts: 6.86 us -> 6.9 us
  transfers between devices with their start and end apart: 7 -> 10, of which waited for: 3 -> 4; matrix products, arithmetic and copies ran while one was open for 15% -> 17% of each run, Pallas kernels for 0% -> 0%
where the time goes in v1:
time: 164 us; the launch traced here: 163 us
  blocking collectives  74.6 us (45%)
  starting transfers between devices  21.5 us (13%)
  waiting for transfers between devices  21.2 us (13%)
  local copies, waits for them, and re-layouts  15 us (9%)
  between operations  14.8 us (9%)
  matrix products  12.6 us (8%)
  other arithmetic  3.38 us (2%)
    all_gather x1, blocking collectives, body(): gathered_key = lax.all_gather(audio_key[0], 'seq', axis=0, tiled=True)  17 us
    unnamed x1, blocking collectives  16.6 us
    all_gather x1, blocking collectives, audio_block(): lax.all_gather(own_features, 'seq', axis=0, tiled=True)  13.9 us
    all_gather x1, blocking collectives, body(): gathered_value = lax.all_gather(audio_value[0], 'seq', axis=0, tiled=True)  13.3 us
    pmax x1, blocking collectives, audio_listen(): peak_value = lax.pmax(local_peak, 'seq')  9.38 us
    all_to_all x1, waiting for transfers between devices, video_self(): lax.all_to_all(spread(values_in), 'seq', split_axis=0, concat_axis=0, til...  7 us
    unnamed x34, local copies, waits for them, and re-layouts  6.9 us
    ppermute x3, starting transfers between devices, turned_line(): shards = [lax.ppermute(shards[0], axis, hops), *shards]  6.05 us
  transfers between devices with their start and end apart: 10, of which 4 were waited for; matrix products, arithmetic and copies ran while one was open for 17% of the time, Pallas kernels for 0%

profile of v1, /device:TPU:0, one launch (start us, length us, event | category | flops | bytes accessed | tf_op | source)
XLA Modules:
  0.0 163.0 jit_solution(1676137985285470547)
XLA Ops:
  7.2 3.1 %collective-permute-start = (bf16[8,1024]{1,0:T(8,128)(2,1)}, bf16[8,1024]{1,0:T(8,128)(2,1)S(1)}, u32[]{:S(2)}, u32[]{:S(2)}) collective-permute-start(bf16[8,1024]{1,0:T(8,128)(2,1)} %bitcast.83), channel_id=1, source_target_pairs={{0,4},{4,8},{8,12},{12,0},{1,5},{5,9},{9,13},{13,1},{2,6},{6,10},{... | collective-permute-start | bytes 49160 | tf_op jit(solution)/shard_map/ppermute | solution.py:16
  10.3 1.9 %copy.100 = bf16[1,16,4,8,512]{4,3,1,2,0:T(8,128)(2,1)} copy(bf16[1,16,4,8,512]{4,3,2,1,0:T(8,128)(2,1)} %bitcast.80) | data formatting | bytes 1048576 | tf_op jit(solution)/shard_map/reshape;squeeze | solution.py:68
  12.2 3.9 %all-to-all-start.1 = ((bf16[4,128,512]{2,1,0:T(8,128)(2,1)}), bf16[4,128,512]{2,1,0:T(8,128)(2,1)S(1)}, u32[]{:S(2)}, u32[]{:S(2)}) async-start(bf16[4,128,512]{2,1,0:T(8,128)(2,1)} %bitcast.72), calls=%async_computation.1 | async-start | bytes 1048576 | tf_op jit(solution)/shard_map/all_to_all | solution.py:69
  16.0 1.2 copy.65
  17.2 2.1 %collective-permute-start.1 = (bf16[8,1024]{1,0:T(8,128)(2,1)S(1)}, bf16[8,1024]{1,0:T(8,128)(2,1)S(1)}, u32[]{:S(2)}, u32[]{:S(2)}) collective-permute-start(bf16[8,1024]{1,0:T(8,128)(2,1)S(1)} %collective-permute-done), channel_id=1, source_target_pairs={{0,4},{4,8},{8,12},{12,0},{1,5},{5,9},{9,13},{13,1},{2,6},{6,10},{... | collective-permute-start | bytes 49160 | tf_op jit(solution)/shard_map/ppermute | solution.py:16
  19.3 17.0 %all-gather = bf16[1,32,1024]{2,1,0:T(8,128)(2,1)S(1)} all-gather(bf16[1,8,1024]{2,1,0:T(8,128)(2,1)} %param.17), channel_id=2, replica_groups=mesh['clips'=2,'seq'=4,'tp'=2,'dp'=2] {'seq'}, dimensions={1}, use_global_device_ids=true | all-gather | bytes 81920 | tf_op jit(solution)/shard_map/all_gather | solution.py:161
  36.3 0.1 reshape.79
  36.5 0.9 collective-permute-start.2
  37.3 0.2 fusion.56
  37.5 1.1 copy.70
  38.7 0.0 copy-start.9
  38.7 0.2 copy.68
  38.9 3.1 %collective-permute-done.2 = bf16[8,1024]{1,0:T(8,128)(2,1)S(1)} collective-permute-done((bf16[8,1024]{1,0:T(8,128)(2,1)S(1)}, bf16[8,1024]{1,0:T(8,128)(2,1)S(1)}, u32[]{:S(2)}, u32[]{:S(2)}) %collective-permute-start.2) | collective-permute-done | bytes 16416 | tf_op jit(solution)/shard_map/ppermute | solution.py:16
  42.1 0.1 reshape.82
  42.3 0.3 fusion.57
  42.6 9.4 %pmax.7 = f32[32,16]{0,1:T(8,128)S(1)} all-reduce(f32[32,16]{0,1:T(8,128)S(1)} %get-tuple-element.56), channel_id=1, replica_groups=mesh['clips'=2,'seq'=4,'tp'=2,'dp'=2] {'seq'}, use_global_device_ids=true, to_apply=%region_5.6 | all-reduce | flops 512 | bytes 4096 | tf_op jit(solution)/shard_map/pmax | solution.py:102
  52.0 0.3 convolution_bitcast_fusion.1
  52.3 0.2 copy.71
  52.5 0.8 reshape.83
  53.2 0.0 reduce-scatter.3.cloned.1.call-update
  53.3 0.1 fusion.32
  53.3 0.4 reshape_squeeze.15
  53.7 0.9 copy.102
  54.6 0.4 reshape_squeeze.17
  55.0 0.9 copy.101
  55.9 0.6 dynamic-slice
  57.1 0.3 fusion.34
  57.4 0.1 copy.72
  57.5 16.6 %all-reduce = f32[32,16]{1,0:T(8,128)S(1)} all-reduce(f32[32,16]{1,0:T(8,128)S(1)} %copy.72), channel_id=5, replica_groups=mesh['clips'=2,'seq'=4,'tp'=2,'dp'=2] {'seq'}, use_global_device_ids=true, to_apply=%region_8.9.clone | all-reduce | flops 512 | bytes 4096
  74.1 0.1 broadcast_in_dim.16
  74.2 0.1 reshape.84
  74.3 3.6 %all-to-all-start = ((bf16[4,128,512]{2,1,0:T(8,128)(2,1)}), bf16[4,128,512]{2,1,0:T(8,128)(2,1)S(1)}, u32[]{:S(2)}, u32[]{:S(2)}) async-start(bf16[4,128,512]{2,1,0:T(8,128)(2,1)} %bitcast.74), calls=%async_computation | async-start | bytes 1048576 | tf_op jit(solution)/shard_map/all_to_all | solution.py:76
  77.9 0.8 divide_convert_fusion
  78.6 0.0 copy-start.4
  78.6 4.4 %all_gather.14 = bf16[8,2048]{1,0:T(8,128)(2,1)S(1)} all-gather(bf16[8,1024]{1,0:T(8,128)(2,1)S(1)} %divide_convert_fusion), channel_id=1, replica_groups=mesh['clips'=2,'seq'=4,'tp'=2,'dp'=2] {'tp'}, dimensions={1}, use_global_device_ids=true | all-gather | bytes 49152 | tf_op jit(solution)/shard_map/all_gather | solution.py:120
  83.1 0.1 multiply_reduce_fusion
  83.2 0.1 fusion.50
  83.3 13.9 %all_gather.15 = bf16[32,1024]{1,0:T(8,128)(2,1)S(1)} all-gather(bf16[8,1024]{1,0:T(8,128)(2,1)S(1)} %fusion.50), channel_id=1, replica_groups=mesh['clips'=2,'seq'=4,'tp'=2,'dp'=2] {'seq'}, dimensions={0}, use_global_device_ids=true | all-gather | bytes 81920 | tf_op jit(solution)/shard_map/all_gather | solution.py:129
  97.2 4.6 %all-to-all-start.2 = ((bf16[4,128,512]{2,1,0:T(8,128)(2,1)}), bf16[4,128,512]{2,1,0:T(8,128)(2,1)S(1)}, u32[]{:S(2)}, u32[]{:S(2)}) async-start(bf16[4,128,512]{2,1,0:T(8,128)(2,1)} %bitcast.73), calls=%async_computation.2 | async-start | bytes 1048576 | tf_op jit(solution)/shard_map/all_to_all | solution.py:77
  101.7 3.7 %fusion.58 = f32[32,2048]{1,0:T(8,128)} fusion(bf16[32,1024]{1,0:T(8,128)(2,1)S(1)} %all_gather.15, bf16[1024,2048]{1,0:T(8,128)(2,1)} %param.24), kind=kOutput, calls=%fused_computation.76 | convolution fusion | flops 134217728 | bytes 4521984 | tf_op jit(solution)/shard_map/dot_general | solution.py:128
  105.4 0.0 all-reduce.3.cloned.1.call-update
  105.5 0.1 reshape.77
  105.6 0.1 reshape_reshape.10
  105.7 0.7 bitcast_reduce_fusion
  106.5 1.9 %copy-done = f32[4,512,512]{2,1,0:T(8,128)} copy-done((f32[4,512,512]{2,1,0:T(8,128)}, f32[4,512,512]{2,1,0:T(8,128)S(1)}, u32[]{:S(2)}) %copy-start) | copy-done | bytes 4194328
  108.4 0.7 fusion.1
  109.1 7.0 %all-to-all-done.2 = bf16[4,128,512]{2,1,0:T(8,128)(2,1)S(1)} async-done(((bf16[4,128,512]{2,1,0:T(8,128)(2,1)}), bf16[4,128,512]{2,1,0:T(8,128)(2,1)S(1)}, u32[]{:S(2)}, u32[]{:S(2)}) %all-to-all-start.2) | async-done | bytes 524320 | tf_op jit(solution)/shard_map/all_to_all | solution.py:77
  116.1 0.1 reshape_reshape.11
  116.2 3.4 %fusion.17 = bf16[512,4,128]{2,0,1:T(8,128)(2,1)S(1)} fusion(f32[4,512,512]{2,1,0:T(8,128)} %copy-done, f32[512,4]{0,1:T(4,128)S(1)} %get-tuple-element.52, bf16[512,4,128]{2,1,0:T(4,128)(2,1)S(1)} %reshape_reshape.11, f32[512,4]{0,1:T(4,128)S(1)} %fusion.1), kind=kOutput, calls=%fused_computation.18 | convolution fusion | flops 272105472 | bytes 5259264 | tf_op jit(solution)/shard_map/while/body/eval_jaxpr/qhk,khd->qhd/dot_general | solution.py:33
  119.6 0.4 copy.63
  120.0 1.0 convert_element_type.56
  121.0 3.5 %all-to-all-start.3 = ((bf16[4,128,512]{2,1,0:T(8,128)(2,1)}), bf16[4,128,512]{2,1,0:T(8,128)(2,1)S(1)}, u32[]{:S(2)}, u32[]{:S(2)}) async-start(bf16[4,128,512]{2,1,0:T(8,128)(2,1)} %convert_element_type.56), calls=%async_computation.3 | async-start | bytes 1048576 | tf_op jit(solution)/shard_map/all_to_all | solution.py:82
  124.5 0.0 reduce-scatter.5.cloned.1.call-start
  124.5 5.8 %all-reduce.3.cloned.1.call-done = f32[32,2048]{1,0:T(8,128)} async-done(((f32[32,2048]{1,0:T(8,128)}), f32[32,2048]{1,0:T(8,128)}) %all-reduce.3.cloned.1.call-update) | async-done | bytes 262160 | tf_op jit(solution)/shard_map/psum | solution.py:133
  130.4 3.7 %fusion.38 = f32[32,1024]{1,0:T(8,128)} fusion(bf16[2048,1024]{1,0:T(8,128)(2,1)} %param.25, f32[32,2048]{1,0:T(8,128)} %all-reduce.3.cloned.1.call-done), kind=kOutput, calls=%fused_computation.41 | convolution fusion | flops 134807552 | bytes 4587520 | tf_op jit(solution)/shard_map/dot_general | solution.py:135
  134.1 0.0 reduce-scatter.5.cloned.1.call-update
  134.1 13.3 %all-gather.1 = bf16[1,32,1024]{2,1,0:T(8,128)(2,1)S(1)} all-gather(bf16[1,8,1024]{2,1,0:T(8,128)(2,1)S(1)} %copy-done.7), channel_id=3, replica_groups=mesh['clips'=2,'seq'=4,'tp'=2,'dp'=2] {'seq'}, dimensions={1}, use_global_device_ids=true | all-gather | bytes 81920 | tf_op jit(solution)/shard_map/all_gather | solution.py:162
  147.4 0.1 reshape.81
  147.5 0.3 fusion.11
  147.8 0.9 copy.74
  148.7 5.2 %reduce-scatter.5.cloned.1.call-done = f32[8,1024]{1,0:T(8,128)} async-done(((f32[32,1024]{1,0:T(8,128)}), f32[8,1024]{1,0:T(8,128)}) %reduce-scatter.5.cloned.1.call-update) | async-done | bytes 32784 | tf_op jit(solution)/shard_map/reduce_scatter | solution.py:134
  153.8 1.4 convert_bitcast_fusion
  155.2 0.3 copy.64
  155.5 1.0 copy.73
  (37 shorter events, 0.1 us)
Async XLA Ops:
  7.2 34.9 %copy-start.5 = (bf16[1,8,1024]{2,1,0:T(8,128)(2,1)S(1)}, bf16[1,8,1024]{2,1,0:T(8,128)(2,1)}, u32[]{:S(2)}) copy-start(bf16[1,8,1024]{2,1,0:T(8,128)(2,1)} %param.19) | copy-start | bytes 49156
  7.2 31.5 %copy-start.3 = (bf16[1,128,1024]{2,1,0:T(8,128)(2,1)S(1)}, bf16[1,128,1024]{2,1,0:T(8,128)(2,1)}, u32[]{:S(2)}) copy-start(bf16[1,128,1024]{2,1,0:T(8,128)(2,1)} %param.20) | copy-start | bytes 786436
  7.2 46.1 %copy-start.1 = (bf16[1,128,2048]{2,1,0:T(8,128)(2,1)S(1)}, bf16[1,128,2048]{2,1,0:T(8,128)(2,1)}, u32[]{:S(2)}) copy-start(bf16[1,128,2048]{2,1,0:T(8,128)(2,1)} %param.14) | copy-start | bytes 1572868
  7.2 10.0 %collective-permute-start = (bf16[8,1024]{1,0:T(8,128)(2,1)}, bf16[8,1024]{1,0:T(8,128)(2,1)S(1)}, u32[]{:S(2)}, u32[]{:S(2)}) collective-permute-start(bf16[8,1024]{1,0:T(8,128)(2,1)} %bitcast.83), channel_id=1, source_target_pairs={{0,4},{4,8},{8,12},{12,0},{1,5},{5,9},{9,13},{13,1},{2,6},{6,10},{... | collective-permute-start | bytes 49160 | tf_op jit(solution)/shard_map/ppermute | solution.py:16
  12.2 62.1 %all-to-all-start.1 = ((bf16[4,128,512]{2,1,0:T(8,128)(2,1)}), bf16[4,128,512]{2,1,0:T(8,128)(2,1)S(1)}, u32[]{:S(2)}, u32[]{:S(2)}) async-start(bf16[4,128,512]{2,1,0:T(8,128)(2,1)} %bitcast.72), calls=%async_computation.1 | async-start | bytes 1048576 | tf_op jit(solution)/shard_map/all_to_all | solution.py:69
  16.0 38.6 %copy-start.2 = (bf16[1,128,2048]{2,1,0:T(8,128)(2,1)S(1)}, bf16[1,128,2048]{2,1,0:T(8,128)(2,1)}, u32[]{:S(2)}) copy-start(bf16[1,128,2048]{2,1,0:T(8,128)(2,1)} %param.15) | copy-start | bytes 1572868
  16.0 61.8 %reduce-scatter.3.cloned.1.call-start = ((), (), s32[]{:S(2)}) async-start(), calls=%async_computation.6 | async-start | bytes 163840 | tf_op jit(solution)/shard_map/reduce_scatter | solution.py:114
  17.2 19.2 %collective-permute-start.1 = (bf16[8,1024]{1,0:T(8,128)(2,1)S(1)}, bf16[8,1024]{1,0:T(8,128)(2,1)S(1)}, u32[]{:S(2)}, u32[]{:S(2)}) collective-permute-start(bf16[8,1024]{1,0:T(8,128)(2,1)S(1)} %collective-permute-done), channel_id=1, source_target_pairs={{0,4},{4,8},{8,12},{12,0},{1,5},{5,9},{9,13},{13,1},{2,6},{6,10},{... | collective-permute-start | bytes 49160 | tf_op jit(solution)/shard_map/ppermute | solution.py:16
  36.5 5.6 %collective-permute-start.2 = (bf16[8,1024]{1,0:T(8,128)(2,1)S(1)}, bf16[8,1024]{1,0:T(8,128)(2,1)S(1)}, u32[]{:S(2)}, u32[]{:S(2)}) collective-permute-start(bf16[8,1024]{1,0:T(8,128)(2,1)S(1)} %collective-permute-done.1), channel_id=1, source_target_pairs={{0,4},{4,8},{8,12},{12,0},{1,5},{5,9},{9,13},{13,1},{2,6},{6,10},{... | collective-permute-start | bytes 49160 | tf_op jit(solution)/shard_map/ppermute | solution.py:16
  38.7 17.2 %copy-start.9 = (u32[32]{0:T(128)S(1)}, u32[32]{0:T(128)}, u32[]{:S(2)}) copy-start(u32[32]{0:T(128)} %constant.105) | copy-start | bytes 388
  38.7 18.4 %copy-start.8 = (f32[2048]{0:T(1024)S(1)}, f32[2048]{0:T(1024)}, u32[]{:S(2)}) copy-start(f32[2048]{0:T(1024)} %param.23) | copy-start | bytes 24580
  42.6 40.5 %copy-start.6 = (bf16[1,8,2048]{2,1,0:T(8,128)(2,1)S(1)}, bf16[1,8,2048]{2,1,0:T(8,128)(2,1)}, u32[]{:S(2)}) copy-start(bf16[1,8,2048]{2,1,0:T(8,128)(2,1)} %param.22) | copy-start | bytes 98308
  74.3 22.9 %all-to-all-start = ((bf16[4,128,512]{2,1,0:T(8,128)(2,1)}), bf16[4,128,512]{2,1,0:T(8,128)(2,1)S(1)}, u32[]{:S(2)}, u32[]{:S(2)}) async-start(bf16[4,128,512]{2,1,0:T(8,128)(2,1)} %bitcast.74), calls=%async_computation | async-start | bytes 1048576 | tf_op jit(solution)/shard_map/all_to_all | solution.py:76
  78.6 27.8 %copy-start.4 = (bf16[8,1024]{1,0:T(8,128)(2,1)}, bf16[8,1024]{1,0:T(8,128)(2,1)S(1)}, u32[]{:S(2)}) copy-start(bf16[8,1024]{1,0:T(8,128)(2,1)S(1)} %divide_convert_fusion) | copy-start | bytes 49156
  97.2 18.9 %all-to-all-start.2 = ((bf16[4,128,512]{2,1,0:T(8,128)(2,1)}), bf16[4,128,512]{2,1,0:T(8,128)(2,1)S(1)}, u32[]{:S(2)}, u32[]{:S(2)}) async-start(bf16[4,128,512]{2,1,0:T(8,128)(2,1)} %bitcast.73), calls=%async_computation.2 | async-start | bytes 1048576 | tf_op jit(solution)/shard_map/all_to_all | solution.py:77
  101.7 28.6 %all-reduce.3.cloned.1.call-start = ((), (), s32[]{:S(2)}) async-start(), calls=%async_computation.7 | async-start | bytes 524288 | tf_op jit(solution)/shard_map/psum | solution.py:133
  106.5 1.9 %copy-start = (f32[4,512,512]{2,1,0:T(8,128)}, f32[4,512,512]{2,1,0:T(8,128)S(1)}, u32[]{:S(2)}) copy-start(f32[4,512,512]{2,1,0:T(8,128)S(1)} %get-tuple-element.53) | copy-start | bytes 12582916
  119.6 14.5 %copy-start.7 = (bf16[1,8,1024]{2,1,0:T(8,128)(2,1)S(1)}, bf16[1,8,1024]{2,1,0:T(8,128)(2,1)}, u32[]{:S(2)}) copy-start(bf16[1,8,1024]{2,1,0:T(8,128)(2,1)} %param.18) | copy-start | bytes 49156
  121.0 34.2 %all-to-all-start.3 = ((bf16[4,128,512]{2,1,0:T(8,128)(2,1)}), bf16[4,128,512]{2,1,0:T(8,128)(2,1)S(1)}, u32[]{:S(2)}, u32[]{:S(2)}) async-start(bf16[4,128,512]{2,1,0:T(8,128)(2,1)} %convert_element_type.56), calls=%async_computation.3 | async-start | bytes 1048576 | tf_op jit(solution)/shard_map/all_to_all | solution.py:82
  124.5 29.3 %reduce-scatter.5.cloned.1.call-start = ((), (), s32[]{:S(2)}) async-start(), calls=%async_computation.8 | async-start | bytes 163840 | tf_op jit(solution)/shard_map/reduce_scatter | solution.py:134
Sparse Core Ops, SparseCore 0:
  53.4 18.2 reduce-scatter.2
  105.6 24.7 all-reduce.2
  134.2 19.5 reduce-scatter.4
